TPU v7x, 32 devices: a whole 2x2x4 slice. The times are simulated.
32 devices in a mesh: row: 4 (over y, x), col: 8 (over z, core).
Axes of the slice: x: 2, y: 2, z: 4, core: 2. Of those that a mesh axis runs over, the one named last changes fastest.
Arguments:
- panel_right: bfloat16 [32, 1536, 128], P('row', 'col'), may hold values from -1 to 1
- factor_inverse: bfloat16 [1536, 1536], replicated, as said below
- ranks: int32 [32], P(('row', 'col')), may hold values from 32 to 128
- owner_map: int32 [32], replicated, may hold values from 0 to 31, each once
- cores: float32 [4, 8, 8, 4, 128, 128], P('row', 'col'), may hold values from -6 to 6
Outputs:
- new_cores: float32 [4, 8, 8, 4, 128, 128], P('row', 'col')
Inputs may be any that keep to these rules, and one draw needn't show every extreme that they name: `factor_inverse`: lower triangular, the inverse of a Cholesky factor.
All inputs are finite; a program needn't handle non-finite values.
Results may differ from a plain program's by a relative error of at most 0.0033.
Values may be sent and summed in bfloat16 or wider, within the bound.
No kernel may reach another device: no remote copies, remote signals or barrier semaphores. Data moves between devices by JAX's collectives and lax.ppermute only.
A program may use at most 128 MiB of HBM per device.

v0:
```python
import jax
import jax.numpy as jnp
from jax import lax
from jax.sharding import PartitionSpec as P


def body(panel_right, factor_inverse, ranks, owner_map, cores):
    n_row = lax.axis_size("row")
    n_col = lax.axis_size("col")
    devices = n_row * n_col
    order = factor_inverse.shape[0]
    width = panel_right.shape[2]
    whole = lax.all_to_all(panel_right, "col", split_axis=0, concat_axis=1, tiled=True)
    solved = jnp.einsum("ij,bjk->bik", factor_inverse, whole, preferred_element_type=jnp.float32)
    column = lax.broadcasted_iota(jnp.int32, (1, 1, width), 2)
    keep = column < ranks.reshape(1, 1, 1)
    panel_left = jnp.where(keep, solved, 0.0).astype(jnp.bfloat16)
    pieces = panel_left.reshape(devices, order // devices, width)
    spread = lax.all_to_all(pieces, ("row", "col"), split_axis=0, concat_axis=0, tiled=True)
    moved = jnp.take(spread, owner_map, axis=0)
    back = lax.all_to_all(moved, ("row", "col"), split_axis=0, concat_axis=0, tiled=True)
    held = back.reshape(1, order, width)
    column_set = lax.all_gather(held, "row", axis=0, tiled=True)
    gram = jnp.einsum(
        "aik,bil->abkl",
        lax.all_gather(held, "col", axis=0, tiled=True),
        column_set,
        preferred_element_type=jnp.float32,
    )
    return cores - gram[None, None]


def solution(mesh):
    return jax.shard_map(
        body,
        mesh=mesh,
        in_specs=(
            P("row", "col", None),
            P(),
            P(("row", "col")),
            P(),
            P("row", "col", None, None, None, None),
        ),
        out_specs=P("row", "col", None, None, None, None),
        check_vma=False,
    )
```

profile of v0, /device:TPU:0, one launch (start us, length us, event | category | flops | bytes accessed | tf_op | source)
XLA Modules:
  0.0 147.6 jit_solution(1991811806430617758)
XLA Ops:
  6.5 6.4 %all-to-all-start = ((bf16[8,192,128]{2,1,0:T(8,128)(2,1)}), bf16[8,192,128]{2,1,0:T(8,128)(2,1)S(1)}, u32[]{:S(2)}, u32[]{:S(2)}) async-start(bf16[8,192,128]{2,1,0:T(8,128)(2,1)} %param.5), calls=%async_computation | async-start | bytes 786432 | tf_op jit(solution)/shard_map/all_to_all | solution.py:13
  13.6 11.9 %all-to-all-done = bf16[8,192,128]{2,1,0:T(8,128)(2,1)S(1)} async-done(((bf16[8,192,128]{2,1,0:T(8,128)(2,1)}), bf16[8,192,128]{2,1,0:T(8,128)(2,1)S(1)}, u32[]{:S(2)}, u32[]{:S(2)}) %all-to-all-start) | async-done | bytes 393248 | tf_op jit(solution)/shard_map/all_to_all | solution.py:13
  25.4 0.0 copy-start
  25.4 4.0 %fusion.4 = bf16[1,1536,128]{1,2,0:T(8,128)(2,1)S(1)} fusion(bf16[1536,128]{1,0:T(8,128)(2,1)S(1)} %bitcast.33, bf16[1536,1536]{1,0:T(8,128)(2,1)} %param.6, pred[128]{0:T(512)(128)(4,1)S(1)} %iota_compare_fusion), kind=kOutput, calls=%fused_computation.6 | convolution fusion | flops 604372992 | bytes 5505152 | tf_op jit(solution)/shard_map/ij,bjk->bik/dot_general | solution.py:14
  29.4 0.9 copy.14
  30.4 3.5 %all-to-all-start.1 = ((bf16[32,48,128]{2,1,0:T(8,128)(2,1)}), bf16[32,48,128]{2,1,0:T(8,128)(2,1)S(1)}, u32[]{:S(2)}, u32[]{:S(2)}) async-start(bf16[32,48,128]{2,1,0:T(8,128)(2,1)} %bitcast.4), calls=%async_computation.1 | async-start | bytes 786432 | tf_op jit(solution)/shard_map/all_to_all | solution.py:19
  33.9 0.0 all-gather.3.cloned.1.call-start
  34.0 0.0 copy-done
  34.0 13.3 %all-to-all-done.1 = bf16[32,48,128]{2,1,0:T(8,128)(2,1)S(1)} async-done(((bf16[32,48,128]{2,1,0:T(8,128)(2,1)}), bf16[32,48,128]{2,1,0:T(8,128)(2,1)S(1)}, u32[]{:S(2)}, u32[]{:S(2)}) %all-to-all-start.1) | async-done | bytes 393248 | tf_op jit(solution)/shard_map/all_to_all | solution.py:19
  47.3 0.6 gather_fusion
  48.0 0.1 broadcast_select_fusion
  48.1 15.8 %all_to_all.19 = bf16[32,48,128]{2,1,0:T(8,128)(2,1)} all-to-all(bf16[32,48,128]{2,1,0:T(8,128)(2,1)S(1)} %broadcast_select_fusion), channel_id=1, replica_groups=mesh['row'=4,'col'=8] {'row','col'}, dimensions={0} | all-to-all | bytes 786432 | tf_op jit(solution)/shard_map/all_to_all | solution.py:21
  63.9 0.0 all-gather.3.cloned.1.call-update
  63.9 0.0 all-gather.5.cloned.1.call-start
  64.0 0.7 all-gather.5.cloned.1.call-update
  64.7 1.9 %copy.16 = f32[1,1,8,4,128,128]{4,5,2,3,1,0:T(8,128)S(1)} copy(f32[1,1,8,4,128,128]{5,4,3,2,1,0:T(8,128)} %param.9) | data formatting | bytes 4194304 | tf_op args[4]
  66.6 25.9 %all-gather.3.cloned.1.call-done = bf16[4,1536,128]{2,1,0:T(8,128)(2,1)} async-done(((bf16[1,1536,128]{2,1,0:T(8,128)(2,1)}), bf16[4,1536,128]{2,1,0:T(8,128)(2,1)}) %all-gather.3.cloned.1.call-update) | async-done | bytes 1572880 | tf_op jit(solution)/shard_map/all_gather | solution.py:23
  92.5 39.9 %all-gather.5.cloned.1.call-done = bf16[8,1536,128]{2,1,0:T(8,128)(2,1)} async-done(((bf16[1,1536,128]{2,1,0:T(8,128)(2,1)}), bf16[8,1536,128]{2,1,0:T(8,128)(2,1)}) %all-gather.5.cloned.1.call-update) | async-done | bytes 3145744 | tf_op jit(solution)/shard_map/all_gather | solution.py:26
  132.4 5.5 %bitcast_subtract_fusion = f32[1,1,8,4,128,128]{4,5,2,3,1,0:T(8,128)} fusion(f32[1,1,8,4,128,128]{4,5,2,3,1,0:T(8,128)S(1)} %copy.16, bf16[8,1536,128]{2,1,0:T(8,128)(2,1)} %all-gather.5.cloned.1.call-done, bf16[4,1536,128]{2,1,0:T(8,128)(2,1)} %all-gather.3.cloned.1.call-done), kind=kOutput, calls=%fused_computation.7 | convolution fusion | flops 1611137024 | bytes 8912896 | tf_op jit(solution)/shard_map/aik,bil->abkl/dot_general | solution.py:24
  137.9 2.9 %copy.17 = f32[1,1,8,4,128,128]{5,4,3,2,1,0:T(8,128)} copy(f32[1,1,8,4,128,128]{4,5,2,3,1,0:T(8,128)} %bitcast_subtract_fusion) | data formatting | bytes 4194304 | tf_op jit(solution)/shard_map/sub | solution.py:30
  (4 shorter events, 0.0 us)
Async XLA Ops:
  6.5 18.9 %all-to-all-start = ((bf16[8,192,128]{2,1,0:T(8,128)(2,1)}), bf16[8,192,128]{2,1,0:T(8,128)(2,1)S(1)}, u32[]{:S(2)}, u32[]{:S(2)}) async-start(bf16[8,192,128]{2,1,0:T(8,128)(2,1)} %param.5), calls=%async_computation | async-start | bytes 786432 | tf_op jit(solution)/shard_map/all_to_all | solution.py:13
  25.4 8.6 %copy-start = (s32[32]{0:T(128)S(1)}, s32[32]{0:T(128)}, u32[]{:S(2)}) copy-start(s32[32]{0:T(128)} %param.8) | copy-start | bytes 388
  30.4 17.0 %all-to-all-start.1 = ((bf16[32,48,128]{2,1,0:T(8,128)(2,1)}), bf16[32,48,128]{2,1,0:T(8,128)(2,1)S(1)}, u32[]{:S(2)}, u32[]{:S(2)}) async-start(bf16[32,48,128]{2,1,0:T(8,128)(2,1)} %bitcast.4), calls=%async_computation.1 | async-start | bytes 786432 | tf_op jit(solution)/shard_map/all_to_all | solution.py:19
  33.9 58.6 %all-gather.3.cloned.1.call-start = ((), (), s32[]{:S(2)}) async-start(), calls=%async_computation.3 | async-start | bytes 1966080 | tf_op jit(solution)/shard_map/all_gather | solution.py:23
  63.9 68.5 %all-gather.5.cloned.1.call-start = ((), (), s32[]{:S(2)}) async-start(), calls=%async_computation.4 | async-start | bytes 3538944 | tf_op jit(solution)/shard_map/all_gather | solution.py:26
Sparse Core Ops, SparseCore 0:
  64.0 28.4 all-gather.2
  94.1 38.2 all-gather.4
where the time goes:
time: 148 us
  waiting for transfers between devices  91.7 us (62%)
  blocking collectives  15.8 us (11%)
  between operations  14.1 us (10%)
  starting transfers between devices  9.97 us (7%)
  matrix products  9.54 us (6%)
  local copies, waits for them, and re-layouts  6.37 us (4%)
    all_gather x1, waiting for transfers between devices, body(): lax.all_gather(held, 'col', axis=0, tiled=True)  39.9 us
    all_gather x1, waiting for transfers between devices, body(): column_set = lax.all_gather(held, 'row', axis=0, tiled=True)  25.9 us
    all_to_all x1, blocking collectives, body(): lax.all_to_all(moved, ('row', 'col'), split_axis=0, concat_axis=0, tiled=...  15.8 us
    all_to_all x1, waiting for transfers between devices, body(): lax.all_to_all(pieces, ('row', 'col'), split_axis=0, concat_axis=0, tiled...  13.3 us
    all_to_all x1, waiting for transfers between devices, body(): lax.all_to_all(panel_right, 'col', split_axis=0, concat_axis=1, tiled=True)  11.9 us
    all_to_all x1, starting transfers between devices, body(): lax.all_to_all(panel_right, 'col', split_axis=0, concat_axis=1, tiled=True)  6.35 us
    dot_general x1, matrix products, body(): jnp.einsum('aik,bil->abkl', lax.all_gather(held, 'col', axis=0, tiled=Tru...  5.51 us
    dot_general x1, matrix products, body(): jnp.einsum('ij,bjk->bik', factor_inverse, whole, preferred_element_type=j...  4.03 us
  transfers between devices with their start and end apart: 4, of which 4 were waited for; matrix products, arithmetic and copies ran while one was open for 1% of the time, Pallas kernels for 0%

commit v1 on v0

--- a/solution.py
+++ b/solution.py
@@ -2,6 +2,31 @@
 import jax.numpy as jnp
 from jax import lax
 from jax.sharding import PartitionSpec as P
+
+
+def in_order(blocks, dim):
+    blocks = jnp.moveaxis(blocks, 0, dim)
+    dims = blocks.shape
+    return blocks.reshape(*dims[:dim], dims[dim] * dims[dim + 1], *dims[dim + 2 :])
+
+
+def work_both_ways(array, axis, dim, apply, out_dim):
+    devices, place, rows = (lax.axis_size(axis), lax.axis_index(axis), array.shape[dim])
+    right = [(i, (i + 1) % devices) for i in range(devices)]
+    downward = [(i, (i - 1) % devices) for i in range(devices)]
+    half = devices // 2
+    tiles = {}
+    from_left = from_right = array
+    for step in range(half + 1):
+        next_left = lax.ppermute(from_left, axis, right) if step < half else None
+        next_right = lax.ppermute(from_right, axis, downward) if step < devices - half - 1 else None
+        tiles[-step] = apply(from_left, (place - step) % devices * rows)
+        if 0 < step < devices - half:
+            tiles[step] = apply(from_right, (place + step) % devices * rows)
+        from_left, from_right = (next_left, next_right)
+    tiles = jnp.stack([tiles[k] for k in sorted(tiles)])
+    tiles = tiles[(jnp.arange(devices) - place + half) % devices]
+    return in_order(tiles, out_dim)
 
 
 def body(panel_right, factor_inverse, ranks, owner_map, cores):
@@ -21,11 +46,14 @@
     back = lax.all_to_all(moved, ("row", "col"), split_axis=0, concat_axis=0, tiled=True)
     held = back.reshape(1, order, width)
     column_set = lax.all_gather(held, "row", axis=0, tiled=True)
-    gram = jnp.einsum(
-        "aik,bil->abkl",
-        lax.all_gather(held, "col", axis=0, tiled=True),
-        column_set,
-        preferred_element_type=jnp.float32,
+    gram = work_both_ways(
+        held,
+        "col",
+        0,
+        lambda shard, start: jnp.einsum(
+            "aik,bil->abkl", shard, column_set, preferred_element_type=jnp.float32
+        ),
+        0,
     )
     return cores - gram[None, None]
 

time: 148 us -> 133 us (0.90)
  waiting for transfers between devices: 91.7 us -> 53 us
  starting transfers between devices: 9.97 us -> 21.1 us
  local copies, waits for them, and re-layouts: 6.37 us -> 11.3 us
  matrix products: 9.54 us -> 13.5 us
  other arithmetic: 0.13 us -> 3.33 us
    all_gather x1 -> x0, waiting for transfers between devices: 39.9 us -> none  [body(): lax.all_gather(held, 'col', axis=0, tiled=True)]
    ppermute x0 -> x7, waiting for transfers between devices: none -> 27.8 us  [the longest x4 22.2 us: work_both_ways(): next_left = lax.ppermute(from_left, axis, right) if step < half else None]
    all_gather x1, waiting for transfers between devices: 25.9 us -> 0.01 us  [body(): column_set = lax.all_gather(held, 'row', axis=0, tiled=True)]
    ppermute x0 -> x7, starting transfers between devices: none -> 11.1 us  [the longest x3 11 us: work_both_ways(): lax.ppermute(from_right, axis, downward)]
    dot_general x1 -> x8, matrix products: 5.51 us -> 9.51 us  [body(): jnp.einsum('aik,bil->abkl', shard, column_set, preferred_element_type=jnp...]
    gather x0 -> x1, local copies, waits for them, and re-layouts: none -> 3.61 us  [work_both_ways(): tiles = tiles[(jnp.arange(devices) - place + half) % devices]]
    sub x0 -> x1, other arithmetic: none -> 3.18 us  [body(): return cores - gram[None, None]]
    unnamed x3 -> x9, local copies, waits for them, and re-layouts: 1.94 us -> 3.24 us
  transfers between devices with their start and end apart: 4 -> 10, of which waited for: 4 -> 8; matrix products, arithmetic and copies ran while one was open for 1% -> 7% of each run, Pallas kernels for 0% -> 0%
where the time goes in v1:
time: 133 us; the launch traced here: 132 us
  waiting for transfers between devices  53 us (40%)
  starting transfers between devices  21.1 us (16%)
  blocking collectives  15.8 us (12%)
  between operations  14.2 us (11%)
  matrix products  13.5 us (10%)
  local copies, waits for them, and re-layouts  11.3 us (8%)
  other arithmetic  3.33 us (3%)
    ppermute x4, waiting for transfers between devices, work_both_ways(): next_left = lax.ppermute(from_left, axis, right) if step < half else None  22.2 us
    all_to_all x1, blocking collectives, body(): lax.all_to_all(moved, ('row', 'col'), split_axis=0, concat_axis=0, tiled=...  15.8 us
    all_to_all x1, waiting for transfers between devices, body(): lax.all_to_all(pieces, ('row', 'col'), split_axis=0, concat_axis=0, tiled...  13.3 us
    all_to_all x1, waiting for transfers between devices, body(): lax.all_to_all(panel_right, 'col', split_axis=0, concat_axis=1, tiled=True)  11.9 us
    ppermute x3, starting transfers between devices, work_both_ways(): lax.ppermute(from_right, axis, downward)  11 us
    dot_general x8, matrix products, body(): jnp.einsum('aik,bil->abkl', shard, column_set, preferred_element_type=jnp...  9.51 us
    all_to_all x1, starting transfers between devices, body(): lax.all_to_all(panel_right, 'col', split_axis=0, concat_axis=1, tiled=True)  6.35 us
    ppermute x3, waiting for transfers between devices, work_both_ways(): lax.ppermute(from_right, axis, downward)  5.64 us
  transfers between devices with their start and end apart: 10, of which 8 were waited for; matrix products, arithmetic and copies ran while one was open for 7% of the time, Pallas kernels for 0%

profile of v1, /device:TPU:0, one launch (start us, length us, event | category | flops | bytes accessed | tf_op | source)
XLA Modules:
  0.0 132.3 jit_solution(15430891487313819241)
XLA Ops:
  6.5 6.4 %all-to-all-start = ((bf16[8,192,128]{2,1,0:T(8,128)(2,1)}), bf16[8,192,128]{2,1,0:T(8,128)(2,1)S(1)}, u32[]{:S(2)}, u32[]{:S(2)}) async-start(bf16[8,192,128]{2,1,0:T(8,128)(2,1)} %param.5), calls=%async_computation | async-start | bytes 786432 | tf_op jit(solution)/shard_map/all_to_all | solution.py:38
  13.6 11.9 %all-to-all-done = bf16[8,192,128]{2,1,0:T(8,128)(2,1)S(1)} async-done(((bf16[8,192,128]{2,1,0:T(8,128)(2,1)}), bf16[8,192,128]{2,1,0:T(8,128)(2,1)S(1)}, u32[]{:S(2)}, u32[]{:S(2)}) %all-to-all-start) | async-done | bytes 393248 | tf_op jit(solution)/shard_map/all_to_all | solution.py:38
  25.4 0.0 copy-start.3
  25.4 4.0 %fusion.2 = bf16[1,1536,128]{1,2,0:T(8,128)(2,1)S(1)} fusion(bf16[1536,128]{1,0:T(8,128)(2,1)S(1)} %bitcast.131, bf16[1536,1536]{1,0:T(8,128)(2,1)} %param.6, pred[128]{0:T(512)(128)(4,1)S(1)} %iota_compare_fusion), kind=kOutput, calls=%fused_computation.5 | convolution fusion | flops 604372992 | bytes 5505152 | tf_op jit(solution)/shard_map/ij,bjk->bik/dot_general | solution.py:39
  29.4 0.9 copy.29
  30.4 3.5 %all-to-all-start.1 = ((bf16[32,48,128]{2,1,0:T(8,128)(2,1)}), bf16[32,48,128]{2,1,0:T(8,128)(2,1)S(1)}, u32[]{:S(2)}, u32[]{:S(2)}) async-start(bf16[32,48,128]{2,1,0:T(8,128)(2,1)} %bitcast.4), calls=%async_computation.1 | async-start | bytes 786432 | tf_op jit(solution)/shard_map/all_to_all | solution.py:44
  33.9 0.0 all-gather.2.cloned.1.call-start
  34.0 0.0 copy-done.3
  34.0 13.3 %all-to-all-done.1 = bf16[32,48,128]{2,1,0:T(8,128)(2,1)S(1)} async-done(((bf16[32,48,128]{2,1,0:T(8,128)(2,1)}), bf16[32,48,128]{2,1,0:T(8,128)(2,1)S(1)}, u32[]{:S(2)}, u32[]{:S(2)}) %all-to-all-start.1) | async-done | bytes 393248 | tf_op jit(solution)/shard_map/all_to_all | solution.py:44
  47.3 0.6 gather_fusion
  48.0 0.1 broadcast_select_fusion
  48.1 15.8 %all_to_all.19 = bf16[32,48,128]{2,1,0:T(8,128)(2,1)} all-to-all(bf16[32,48,128]{2,1,0:T(8,128)(2,1)S(1)} %broadcast_select_fusion), channel_id=1, replica_groups=mesh['row'=4,'col'=8] {'row','col'}, dimensions={0} | all-to-all | bytes 786432 | tf_op jit(solution)/shard_map/all_to_all | solution.py:46
  63.9 0.0 all-gather.2.cloned.1.call-update
  63.9 0.2 collective-permute-start
  64.1 9.1 %collective-permute-done = bf16[1,1536,128]{2,1,0:T(8,128)(2,1)S(1)} collective-permute-done((bf16[1,1536,128]{2,1,0:T(8,128)(2,1)}, bf16[1,1536,128]{2,1,0:T(8,128)(2,1)S(1)}, u32[]{:S(2)}, u32[]{:S(2)}) %collective-permute-start) | collective-permute-done | bytes 393248 | tf_op jit(solution)/shard_map/ppermute | solution.py:21
  73.2 0.0 collective-permute-start.1
  73.2 3.5 %collective-permute-start.4 = (bf16[1,1536,128]{2,1,0:T(8,128)(2,1)}, bf16[1,1536,128]{2,1,0:T(8,128)(2,1)S(1)}, u32[]{:S(2)}, u32[]{:S(2)}) collective-permute-start(bf16[1,1536,128]{2,1,0:T(8,128)(2,1)} %bitcast.128), channel_id=1, source_target_pairs={{0,7},{1,0},{2,1},{3,2},{4,3},{5,4},{6,5},{7,6},{8,15},{9,8},{10,9... | collective-permute-start | bytes 1179656 | tf_op jit(solution)/shard_map/ppermute | solution.py:22
  76.7 6.5 %collective-permute-done.1 = bf16[1,1536,128]{2,1,0:T(8,128)(2,1)S(1)} collective-permute-done((bf16[1,1536,128]{2,1,0:T(8,128)(2,1)S(1)}, bf16[1,1536,128]{2,1,0:T(8,128)(2,1)S(1)}, u32[]{:S(2)}, u32[]{:S(2)}) %collective-permute-start.1) | collective-permute-done | bytes 393248 | tf_op jit(solution)/shard_map/ppermute | solution.py:21
  83.2 0.0 collective-permute-start.2
  83.2 2.3 %collective-permute-done.4 = bf16[1,1536,128]{2,1,0:T(8,128)(2,1)S(1)} collective-permute-done((bf16[1,1536,128]{2,1,0:T(8,128)(2,1)}, bf16[1,1536,128]{2,1,0:T(8,128)(2,1)S(1)}, u32[]{:S(2)}, u32[]{:S(2)}) %collective-permute-start.4) | collective-permute-done | bytes 393248 | tf_op jit(solution)/shard_map/ppermute | solution.py:22
  85.6 3.6 %collective-permute-start.5 = (bf16[1,1536,128]{2,1,0:T(8,128)(2,1)S(1)}, bf16[1,1536,128]{2,1,0:T(8,128)(2,1)}, u32[]{:S(2)}, u32[]{:S(2)}) collective-permute-start(bf16[1,1536,128]{2,1,0:T(8,128)(2,1)S(1)} %collective-permute-done.4), channel_id=1, source_target_pairs={{0,7},{1,0},{2,1},{3,2},{4,3},{5,4},{6,5},{7,6},{8,15},{9,8},{10,9... | collective-permute-start | bytes 1179656 | tf_op jit(solution)/shard_map/ppermute | solution.py:22
  89.2 3.8 %collective-permute-done.2 = bf16[1,1536,128]{2,1,0:T(8,128)(2,1)} collective-permute-done((bf16[1,1536,128]{2,1,0:T(8,128)(2,1)S(1)}, bf16[1,1536,128]{2,1,0:T(8,128)(2,1)}, u32[]{:S(2)}, u32[]{:S(2)}) %collective-permute-start.2) | collective-permute-done | bytes 393248 | tf_op jit(solution)/shard_map/ppermute | solution.py:21
  93.0 0.0 collective-permute-start.3
  93.0 1.9 %copy.38 = f32[1,1,8,4,128,128]{4,5,3,2,1,0:T(8,128)S(1)} copy(f32[1,1,8,4,128,128]{5,4,3,2,1,0:T(8,128)} %param.9) | data formatting | bytes 4194304 | tf_op args[4]
  94.9 3.3 %collective-permute-done.5 = bf16[1,1536,128]{2,1,0:T(8,128)(2,1)} collective-permute-done((bf16[1,1536,128]{2,1,0:T(8,128)(2,1)S(1)}, bf16[1,1536,128]{2,1,0:T(8,128)(2,1)}, u32[]{:S(2)}, u32[]{:S(2)}) %collective-permute-start.5) | collective-permute-done | bytes 393248 | tf_op jit(solution)/shard_map/ppermute | solution.py:22
  98.2 3.8 %collective-permute-start.6 = (bf16[1,1536,128]{2,1,0:T(8,128)(2,1)}, bf16[1,1536,128]{2,1,0:T(8,128)(2,1)}, u32[]{:S(2)}, u32[]{:S(2)}) collective-permute-start(bf16[1,1536,128]{2,1,0:T(8,128)(2,1)} %collective-permute-done.5), channel_id=1, source_target_pairs={{0,7},{1,0},{2,1},{3,2},{4,3},{5,4},{6,5},{7,6},{8,15},{9,8},{10,9... | collective-permute-start | bytes 1179656 | tf_op jit(solution)/shard_map/ppermute | solution.py:22
  102.0 2.8 %collective-permute-done.3 = bf16[1,1536,128]{2,1,0:T(8,128)(2,1)} collective-permute-done((bf16[1,1536,128]{2,1,0:T(8,128)(2,1)}, bf16[1,1536,128]{2,1,0:T(8,128)(2,1)}, u32[]{:S(2)}, u32[]{:S(2)}) %collective-permute-start.3) | collective-permute-done | bytes 393248 | tf_op jit(solution)/shard_map/ppermute | solution.py:21
  104.8 0.0 all-gather.2.cloned.1.call-done
  104.8 0.0 copy-start
  104.8 2.2 %fusion.10 = f32[8,1,4,128,128]{3,4,2,1,0:T(8,128)S(1)} fusion(bf16[4,1536,128]{2,1,0:T(8,128)(2,1)} %all-gather.2.cloned.1.call-done, bf16[1,1536,128]{2,1,0:T(8,128)(2,1)} %collective-permute-done.3), kind=kOutput, calls=%fused_computation.22 | convolution fusion | flops 201326592 | bytes 2228224 | tf_op jit(solution)/shard_map/aik,bil->abkl/dot_general | solution.py:53
  107.0 0.0 copy-done
  107.0 1.6 %fusion.9 = f32[8,1,4,128,128]{3,4,2,1,0:T(8,128)S(1)} fusion(f32[8,1,4,128,128]{3,4,2,1,0:T(8,128)S(1)} %fusion.10, bf16[4,1536,128]{2,1,0:T(8,128)(2,1)S(1)} %copy-done, bf16[1,1536,128]{2,1,0:T(8,128)(2,1)} %collective-permute-done.2), kind=kOutput, calls=%fused_computation.20 | convolution fusion | flops 201326592 | bytes 2228224 | tf_op jit(solution)/shard_map/aik,bil->abkl/dot_general | solution.py:53
  108.7 0.0 copy-start.1
  108.7 0.6 fusion.8
  109.3 0.6 fusion.7
  109.9 0.0 copy-done.1
  109.9 0.6 fusion.6
  110.6 0.6 fusion.5
  111.2 1.6 %fusion.4 = f32[8,1,4,128,128]{3,4,2,1,0:T(8,128)S(1)} fusion(f32[8,1,4,128,128]{3,4,2,1,0:T(8,128)S(1)} %fusion.5, bf16[4,1536,128]{2,1,0:T(8,128)(2,1)S(1)} %copy-done, bf16[1,1536,128]{2,1,0:T(8,128)(2,1)} %collective-permute-done.5), kind=kOutput, calls=%fused_computation.10 | convolution fusion | flops 201326592 | bytes 2228224 | tf_op jit(solution)/shard_map/aik,bil->abkl/dot_general | solution.py:53
  112.8 0.0 collective-permute-done.6
  112.8 1.6 %fusion.3 = f32[8,1,4,128,128]{3,4,2,1,0:T(8,128)S(1)} fusion(f32[8,1,4,128,128]{3,4,2,1,0:T(8,128)S(1)} %fusion.4, bf16[4,1536,128]{2,1,0:T(8,128)(2,1)S(1)} %copy-done, bf16[1,1536,128]{2,1,0:T(8,128)(2,1)} %collective-permute-done.6), kind=kOutput, calls=%fused_computation.8 | convolution fusion | flops 201326592 | bytes 2228224 | tf_op jit(solution)/shard_map/aik,bil->abkl/dot_general | solution.py:53
  114.4 0.0 copy-start.2
  114.4 1.3 copy-done.2
  115.8 3.6 %gather_fusion.1 = f32[8,4,128,128]{2,3,1,0:T(8,128)} fusion(f32[8,4,128,128]{2,3,1,0:T(8,128)} %bitcast.130, s32[1024]{0:T(1024)S(1)} %pad_clamp_fusion), kind=kCustom, calls=%fused_computation.1 | custom fusion | bytes 4194336 | tf_op jit(solution)/shard_map/gather | solution.py:28
  119.4 3.2 %bitcast_subtract_fusion = f32[1,1,8,4,128,128]{4,5,3,2,1,0:T(8,128)} fusion(f32[1,1,8,4,128,128]{4,5,3,2,1,0:T(8,128)S(1)} %copy.38, f32[8,4,128,128]{2,3,1,0:T(8,128)} %gather_fusion.1), kind=kLoop, calls=%fused_computation.6 | loop fusion | flops 524288 | bytes 6291456 | tf_op jit(solution)/shard_map/sub | solution.py:58
  122.5 2.9 %copy.39 = f32[1,1,8,4,128,128]{5,4,3,2,1,0:T(8,128)} copy(f32[1,1,8,4,128,128]{4,5,3,2,1,0:T(8,128)} %bitcast_subtract_fusion) | data formatting | bytes 4194304 | tf_op jit(solution)/shard_map/sub | solution.py:58
  (6 shorter events, 0.0 us)
Async XLA Ops:
  6.5 18.9 %all-to-all-start = ((bf16[8,192,128]{2,1,0:T(8,128)(2,1)}), bf16[8,192,128]{2,1,0:T(8,128)(2,1)S(1)}, u32[]{:S(2)}, u32[]{:S(2)}) async-start(bf16[8,192,128]{2,1,0:T(8,128)(2,1)} %param.5), calls=%async_computation | async-start | bytes 786432 | tf_op jit(solution)/shard_map/all_to_all | solution.py:38
  25.4 8.6 %copy-start.3 = (s32[32]{0:T(128)S(1)}, s32[32]{0:T(128)}, u32[]{:S(2)}) copy-start(s32[32]{0:T(128)} %param.8) | copy-start | bytes 388
  30.4 17.0 %all-to-all-start.1 = ((bf16[32,48,128]{2,1,0:T(8,128)(2,1)}), bf16[32,48,128]{2,1,0:T(8,128)(2,1)S(1)}, u32[]{:S(2)}, u32[]{:S(2)}) async-start(bf16[32,48,128]{2,1,0:T(8,128)(2,1)} %bitcast.4), calls=%async_computation.1 | async-start | bytes 786432 | tf_op jit(solution)/shard_map/all_to_all | solution.py:44
  33.9 70.9 %all-gather.2.cloned.1.call-start = ((), (), s32[]{:S(2)}) async-start(), calls=%async_computation.3 | async-start | bytes 1966080 | tf_op jit(solution)/shard_map/all_gather | solution.py:48
  63.9 9.3 %collective-permute-start = (bf16[1,1536,128]{2,1,0:T(8,128)(2,1)}, bf16[1,1536,128]{2,1,0:T(8,128)(2,1)S(1)}, u32[]{:S(2)}, u32[]{:S(2)}) collective-permute-start(bf16[1,1536,128]{2,1,0:T(8,128)(2,1)} %bitcast.127), channel_id=1, source_target_pairs={{0,1},{1,2},{2,3},{3,4},{4,5},{5,6},{6,7},{7,0},{8,9},{9,10},{10,1... | collective-permute-start | bytes 1179656 | tf_op jit(solution)/shard_map/ppermute | solution.py:21
  73.2 10.0 %collective-permute-start.1 = (bf16[1,1536,128]{2,1,0:T(8,128)(2,1)S(1)}, bf16[1,1536,128]{2,1,0:T(8,128)(2,1)S(1)}, u32[]{:S(2)}, u32[]{:S(2)}) collective-permute-start(bf16[1,1536,128]{2,1,0:T(8,128)(2,1)S(1)} %collective-permute-done), channel_id=1, source_target_pairs={{0,1},{1,2},{2,3},{3,4},{4,5},{5,6},{6,7},{7,0},{8,9},{9,10},{10,1... | collective-permute-start | bytes 1179656 | tf_op jit(solution)/shard_map/ppermute | solution.py:21
  73.2 12.4 %collective-permute-start.4 = (bf16[1,1536,128]{2,1,0:T(8,128)(2,1)}, bf16[1,1536,128]{2,1,0:T(8,128)(2,1)S(1)}, u32[]{:S(2)}, u32[]{:S(2)}) collective-permute-start(bf16[1,1536,128]{2,1,0:T(8,128)(2,1)} %bitcast.128), channel_id=1, source_target_pairs={{0,7},{1,0},{2,1},{3,2},{4,3},{5,4},{6,5},{7,6},{8,15},{9,8},{10,9... | collective-permute-start | bytes 1179656 | tf_op jit(solution)/shard_map/ppermute | solution.py:22
  83.2 9.8 %collective-permute-start.2 = (bf16[1,1536,128]{2,1,0:T(8,128)(2,1)S(1)}, bf16[1,1536,128]{2,1,0:T(8,128)(2,1)}, u32[]{:S(2)}, u32[]{:S(2)}) collective-permute-start(bf16[1,1536,128]{2,1,0:T(8,128)(2,1)S(1)} %collective-permute-done.1), channel_id=1, source_target_pairs={{0,1},{1,2},{2,3},{3,4},{4,5},{5,6},{6,7},{7,0},{8,9},{9,10},{10,1... | collective-permute-start | bytes 1179656 | tf_op jit(solution)/shard_map/ppermute | solution.py:21
  85.6 12.7 %collective-permute-start.5 = (bf16[1,1536,128]{2,1,0:T(8,128)(2,1)S(1)}, bf16[1,1536,128]{2,1,0:T(8,128)(2,1)}, u32[]{:S(2)}, u32[]{:S(2)}) collective-permute-start(bf16[1,1536,128]{2,1,0:T(8,128)(2,1)S(1)} %collective-permute-done.4), channel_id=1, source_target_pairs={{0,7},{1,0},{2,1},{3,2},{4,3},{5,4},{6,5},{7,6},{8,15},{9,8},{10,9... | collective-permute-start | bytes 1179656 | tf_op jit(solution)/shard_map/ppermute | solution.py:22
  93.0 11.9 %collective-permute-start.3 = (bf16[1,1536,128]{2,1,0:T(8,128)(2,1)}, bf16[1,1536,128]{2,1,0:T(8,128)(2,1)}, u32[]{:S(2)}, u32[]{:S(2)}) collective-permute-start(bf16[1,1536,128]{2,1,0:T(8,128)(2,1)} %collective-permute-done.2), channel_id=1, source_target_pairs={{0,1},{1,2},{2,3},{3,4},{4,5},{5,6},{6,7},{7,0},{8,9},{9,10},{10,1... | collective-permute-start | bytes 1179656 | tf_op jit(solution)/shard_map/ppermute | solution.py:21
  98.2 14.6 %collective-permute-start.6 = (bf16[1,1536,128]{2,1,0:T(8,128)(2,1)}, bf16[1,1536,128]{2,1,0:T(8,128)(2,1)}, u32[]{:S(2)}, u32[]{:S(2)}) collective-permute-start(bf16[1,1536,128]{2,1,0:T(8,128)(2,1)} %collective-permute-done.5), channel_id=1, source_target_pairs={{0,7},{1,0},{2,1},{3,2},{4,3},{5,4},{6,5},{7,6},{8,15},{9,8},{10,9... | collective-permute-start | bytes 1179656 | tf_op jit(solution)/shard_map/ppermute | solution.py:22
  104.8 2.2 %copy-start = (bf16[4,1536,128]{2,1,0:T(8,128)(2,1)S(1)}, bf16[4,1536,128]{2,1,0:T(8,128)(2,1)}, u32[]{:S(2)}) copy-start(bf16[4,1536,128]{2,1,0:T(8,128)(2,1)} %all-gather.2.cloned.1.call-done) | copy-start | bytes 4718596
  108.7 1.3 copy-start.1
  114.4 1.3 copy-start.2
Sparse Core Ops, SparseCore 0:
  64.0 28.4 all-gather.1
